TPU v7x, 32 devices: a whole 2x2x4 slice. The times are simulated.
32 devices in a mesh: groups: 2 (over x), blk: 16 (over z, y, core).
Axes of the slice: x: 2, y: 2, z: 4, core: 2. Of those that a mesh axis runs over, the one named last changes fastest.
Arguments:
- text_queries: bfloat16 [4096, 4096], P(('groups', 'blk')), parts along dimension 0, may hold values from -170 to 170
- image_states: bfloat16 [1536, 8192], P(('groups', 'blk')), parts along dimension 0, may hold values from -6 to 6
- kv_weight: bfloat16 [8192, 1024], P('blk'), may hold values from -0.1875 to 0.1875
- q_gain: float32 [128], replicated, may hold values from 0.25 to 1.75
- k_gain: float32 [128], replicated, may hold values from 0.25 to 1.75
- text_counts: int32 [6], P('groups'), parts along dimension 0, may hold values from 1 to 1024, 2048 in all
- image_counts: int32 [6], P('groups'), parts along dimension 0, may hold values from 96 to 384, as said below
Outputs:
- attended: bfloat16 [4096, 4096], P(('groups', 'blk')), parts along dimension 0
There are 2 independent parts, one for each index of `groups`. A program takes and returns all parts, laid end to end along the dimension named above; an argument that names none is the same for every part. Nothing has to cross between parts.
Inputs may be any that keep to these rules, and one draw needn't show every extreme that they name: `text_counts`: they sum to 2048. `image_counts`: they sum to 768; the second image has exactly 384 tokens, the first and last are cut by the window.
All inputs are finite; a program needn't handle non-finite values.
Results may differ from a plain program's by a relative error of at most 0.0071.
Values may be sent and summed in bfloat16 or wider, within the bound.
No kernel may reach another device: no remote copies, remote signals or barrier semaphores. Data moves between devices by JAX's collectives and lax.ppermute only.
A program may use at most 128 MiB of HBM per device.

v0:
```python
import math
import jax
import jax.numpy as jnp
from jax import lax
from jax.sharding import PartitionSpec as P

epsilon = 1e-05


def rms_norm(inputs, norm_gain):
    return (
        inputs * lax.rsqrt(jnp.mean(inputs * inputs, axis=-1, keepdims=True) + epsilon) * norm_gain
    )


def body(text_queries, image_states, kv_weight, q_gain, k_gain, text_counts, image_counts):
    head_dim = q_gain.shape[0]
    text_rows = text_queries.shape[0]
    image_rows = image_states.shape[0]
    kv_width = kv_weight.shape[1] // 2
    kv_heads = kv_width // head_dim
    query_heads = text_queries.shape[1] // head_dim
    group_size = query_heads // kv_heads
    columns = lax.all_to_all(image_states, "blk", split_axis=1, concat_axis=0, tiled=True)
    projected = lax.psum_scatter(
        jnp.dot(columns, kv_weight, preferred_element_type=jnp.float32),
        "blk",
        scatter_dimension=0,
        tiled=True,
    )
    image_keys = rms_norm(projected[:, :kv_width].reshape(image_rows, kv_heads, head_dim), k_gain)
    image_keys = image_keys.astype(jnp.bfloat16).reshape(image_rows, kv_width)
    image_values = projected[:, kv_width:].astype(jnp.bfloat16)
    kv_rows_local = jnp.concatenate([image_keys, image_values], axis=1)
    normed_queries = rms_norm(
        text_queries.astype(jnp.float32).reshape(text_rows, query_heads, head_dim), q_gain
    )
    normed_queries = normed_queries.astype(jnp.bfloat16).reshape(
        text_rows, kv_heads, group_size, head_dim
    )
    text_positions = lax.axis_index("blk") * text_rows + jnp.arange(text_rows, dtype=jnp.int32)
    text_ends = jnp.cumsum(text_counts)
    image_ends = jnp.cumsum(image_counts)
    text_segment = jnp.sum(
        (text_ends[None, :] <= text_positions[:, None]).astype(jnp.int32), axis=1
    )
    score_scale = 1.0 / math.sqrt(head_dim)
    arrived = lax.all_gather(kv_rows_local, "blk", axis=0, tiled=True)
    first_row = jnp.int32(0)
    numerator = jnp.zeros((kv_heads, group_size, text_rows, head_dim), jnp.float32)
    denominator = jnp.zeros((kv_heads, group_size, text_rows), jnp.float32)
    key_span = arrived.shape[0]
    for offset in range(0, key_span, 512):
        block_size = min(512, key_span - offset)
        key_block = arrived[offset : offset + block_size]
        key_heads = key_block[:, :kv_width].reshape(block_size, kv_heads, head_dim)
        value_heads = key_block[:, kv_width:].reshape(block_size, kv_heads, head_dim)
        key_positions = first_row + offset + jnp.arange(block_size, dtype=jnp.int32)
        key_owner = jnp.sum(
            (image_ends[None, :] <= key_positions[:, None]).astype(jnp.int32), axis=1
        )
        allowed = key_owner[None, :] <= text_segment[:, None]
        scores = (
            jnp.einsum(
                "tgrd,pgd->grtp", normed_queries, key_heads, preferred_element_type=jnp.float32
            )
            * score_scale
        )
        weights = jnp.where(allowed, jnp.exp(scores), 0.0)
        denominator = denominator + jnp.sum(weights, axis=-1)
        numerator = numerator + jnp.einsum(
            "grtp,pgd->grtd",
            weights.astype(jnp.bfloat16),
            value_heads,
            preferred_element_type=jnp.float32,
        )
    numerator, denominator = (numerator, denominator)
    attended = (numerator / denominator[..., None]).astype(jnp.bfloat16)
    return jnp.transpose(attended, (2, 0, 1, 3)).reshape(text_rows, query_heads * head_dim)


def solution(mesh):
    placed = (
        P(("groups", "blk"), None),
        P(("groups", "blk"), None),
        P("blk", None),
        P(),
        P(),
        P("groups"),
        P("groups"),
    )
    return jax.shard_map(
        body, mesh=mesh, in_specs=placed, out_specs=P(("groups", "blk"), None), check_vma=False
    )
```

profile of v0, /device:TPU:0, one launch (start us, length us, event | category | flops | bytes accessed | tf_op | source)
XLA Modules:
  0.0 173.4 jit_solution(13814516155407754564)
XLA Ops:
  6.5 1.3 copy.124
  7.8 27.3 %all_to_all.19 = bf16[48,16,512]{2,0,1:T(8,128)(2,1)S(1)} all-to-all(bf16[48,16,512]{2,0,1:T(8,128)(2,1)S(1)} %bitcast.70), channel_id=1, replica_groups=mesh['groups'=2,'blk'=16] {'blk'}, dimensions={1} | all-to-all | bytes 1572864 | tf_op jit(solution)/shard_map/all_to_all | solution.py:24
  35.2 2.6 %fusion.34 = f32[768,1024]{1,0:T(8,128)} fusion(bf16[768,512]{1,0:T(8,128)(2,1)S(1)} %bitcast.69, bf16[512,1024]{1,0:T(8,128)(2,1)S(1)} %copy-done), kind=kOutput, calls=%fused_computation.51 | convolution fusion | flops 805306368 | bytes 4980736 | tf_op jit(solution)/shard_map/dot_general | solution.py:26
  37.9 0.6 copy-done.4
  38.5 65.1 %reduce-scatter.2.cloned.1.call-done = f32[48,1024]{1,0:T(8,128)} async-done(((f32[768,1024]{1,0:T(8,128)}), f32[48,1024]{1,0:T(8,128)}) %reduce-scatter.2.cloned.1.call-update) | async-done | bytes 196624 | tf_op jit(solution)/shard_map/reduce_scatter | solution.py:25
  103.6 0.9 slice_multiply_fusion
  104.5 0.1 reduce_sum.65
  104.7 0.9 slice.40
  105.7 0.9 fusion.27
  106.6 0.6 pad_maximum_fusion
  107.3 0.2 reduce-window.17
  107.5 0.2 reduce-window.16
  107.7 0.2 fusion.9
  107.9 0.4 copy.101
  108.3 0.6 reduce_sum.66
  108.9 1.4 convert_bitcast_fusion
  110.4 0.4 copy.100
  111.0 0.1 broadcast_compare_fusion.1
  111.2 0.1 broadcast_compare_fusion
  111.3 34.7 %all-gather.2.cloned.1.call-done = bf16[768,1024]{1,0:T(8,128)(2,1)} async-done(((bf16[48,1024]{1,0:T(8,128)(2,1)}), bf16[768,1024]{1,0:T(8,128)(2,1)}) %all-gather.2.cloned.1.call-update) | async-done | bytes 1572880 | tf_op jit(solution)/shard_map/all_gather | solution.py:48
  146.0 2.2 %fusion.32 = (bf16[512,512]{1,0:T(8,128)(2,1)}, bf16[512,512]{1,0:T(8,128)(2,1)}) fusion(bf16[768,1024]{1,0:T(8,128)(2,1)} %all-gather.2.cloned.1.call-done), kind=kLoop, calls=%fused_computation.49 | loop fusion | bytes 2097152 | tf_op jit(solution)/shard_map/slice | solution.py:56
  148.3 2.0 %reshape.123 = bf16[512,4,128]{2,1,0:T(4,128)(2,1)} reshape(bf16[512,512]{1,0:T(8,128)(2,1)} %get-tuple-element.5) | data formatting | bytes 1048576 | tf_op jit(solution)/shard_map/reshape | solution.py:56
  150.2 1.8 %fusion.33 = (bf16[256,512]{1,0:T(8,128)(2,1)S(1)}, bf16[256,512]{1,0:T(8,128)(2,1)}) fusion(bf16[768,1024]{1,0:T(8,128)(2,1)} %all-gather.2.cloned.1.call-done), kind=kLoop, calls=%fused_computation.50 | loop fusion | bytes 1048576 | tf_op jit(solution)/shard_map/slice | solution.py:56
  152.0 0.8 reshape.126
  152.8 1.1 copy.97
  153.9 2.0 %copy.94 = bf16[512,512]{0,1:T(8,128)(2,1)} copy(bf16[512,512]{1,0:T(8,128)(2,1)} %get-tuple-element.6) | data formatting | bytes 1048576 | tf_op jit(solution)/shard_map/reshape | solution.py:57
  155.9 3.2 %fusion.7 = (f32[4,8,128]{2,1,0:T(8,128)S(1)}, f32[4,256,128,8]{2,1,3,0:T(8,128)S(1)}) fusion(pred[128,256]{0,1:T(8,128)(4,1)S(1)} %broadcast_compare_fusion.1, f32[128,4,8,128]{3,2,1,0:T(8,128)S(1)} %bitcast.71, f32[128]{0:T(128)S(1)} %copy-done.7, f32[128,4,8]{0,2,1:T(8,128)S(1)} %rsqrt_bitcast_fusion, bf16[256,4,128,1]{2,1,0,3:T(4,128)(2,1)} %bitcast.79), kind=kOutput, calls=%fused_computation.8 | convolution fusion | flops 273149952 | bytes 6619648 | tf_op jit(solution)/shard_map/tgrd,pgd->grtp/dot_general | solution.py:64
  159.1 0.9 fusion.10
  160.0 0.2 copy-done.2
  160.2 3.3 %fusion = (f32[4,8,128]{2,1,0:T(8,128)S(1)}, f32[4,512,128,8]{2,1,3,0:T(8,128)S(1)}) fusion(pred[128,512]{0,1:T(8,128)(4,1)S(1)} %broadcast_compare_fusion, f32[128,4,8,128]{3,2,1,0:T(8,128)S(1)} %bitcast.72, f32[128]{0:T(128)S(1)} %copy-done.7, f32[128,4,8]{0,2,1:T(8,128)S(1)} %rsqrt_bitcast_fusion, bf16[512,4,128,1]{2,1,0,3:T(4,128)(2,1)S(1)} %bitcast.76), kind=kOutput, calls=%fused_computation.1 | convolution fusion | flops 544731136 | bytes 11108864 | tf_op jit(solution)/shard_map/tgrd,pgd->grtp/dot_general | solution.py:64
  163.5 1.8 %fusion.12 = bf16[128,4,8,128]{0,3,2,1:T(8,128)(2,1)S(1)} fusion(f32[4,8,128,128]{2,3,1,0:T(8,128)S(1)} %fusion.10, bf16[512,4,128,1]{0,2,3,1:T(8,128)(2,1)S(1)} %bitcast.77, f32[4,512,128,8]{2,1,3,0:T(8,128)S(1)} %get-tuple-element.10, pred[128,512]{0,1:T(8,128)(4,1)S(1)} %broadcast_compare_fusion, f32[128,4,8]{0,2,1:T(8,128)S(1)} %add_bitcast_fusion), kind=kOutput, calls=%fused_computation.15 | convolution fusion | flops 544735232 | bytes 12140544 | tf_op jit(solution)/shard_map/grtp,pgd->grtd/dot_general | solution.py:71
  165.3 1.3 copy.85
  (30 shorter events, 0.6 us)
Async XLA Ops:
  6.5 28.6 %copy-start = (bf16[512,1024]{1,0:T(8,128)(2,1)S(1)}, bf16[512,1024]{1,0:T(8,128)(2,1)}, u32[]{:S(2)}) copy-start(bf16[512,1024]{1,0:T(8,128)(2,1)} %param.9) | copy-start | bytes 3145732
  6.5 97.0 %reduce-scatter.2.cloned.1.call-start = ((), (), s32[]{:S(2)}) async-start(), calls=%async_computation.2 | async-start | bytes 3342336 | tf_op jit(solution)/shard_map/reduce_scatter | solution.py:25
  37.8 0.7 copy-start.4
  37.8 69.5 %copy-start.5 = (s32[3]{0:T(128)S(1)}, s32[3]{0:T(128)}, u32[]{:S(2)}) copy-start(s32[3]{0:T(128)} %param.12) | copy-start | bytes 40
  37.8 69.6 %copy-start.6 = (s32[3]{0:T(128)S(1)}, s32[3]{0:T(128)}, u32[]{:S(2)}) copy-start(s32[3]{0:T(128)} %param.13) | copy-start | bytes 40
  37.8 69.8 %copy-start.1 = (bf16[128,4096]{1,0:T(8,128)(2,1)S(1)}, bf16[128,4096]{1,0:T(8,128)(2,1)}, u32[]{:S(2)}) copy-start(bf16[128,4096]{1,0:T(8,128)(2,1)} %param.7) | copy-start | bytes 3145732
  37.9 108.2 %all-gather.2.cloned.1.call-start = ((), (), s32[]{:S(2)}) async-start(), calls=%async_computation.3 | async-start | bytes 1671168 | tf_op jit(solution)/shard_map/all_gather | solution.py:48
  148.3 7.7 %copy-start.7 = (f32[128]{0:T(128)S(1)}, f32[128]{0:T(128)}, u32[]{:S(2)}) copy-start(f32[128]{0:T(128)} %param.10) | copy-start | bytes 1540
  159.1 1.0 copy-start.2
  160.2 3.3 %copy-start.3 = (bf16[512,512]{0,1:T(8,128)(2,1)S(1)}, bf16[512,512]{0,1:T(8,128)(2,1)}, u32[]{:S(2)}) copy-start(bf16[512,512]{0,1:T(8,128)(2,1)} %copy.94) | copy-start | bytes 1572868
Sparse Core Ops, SparseCore 0:
  38.0 65.5 reduce-scatter.1
  107.4 38.5 all-gather.1
where the time goes:
time: 174 us; the launch traced here: 173 us
  waiting for transfers between devices  99.9 us (57%)
  blocking collectives  27.3 us (16%)
  local copies, waits for them, and re-layouts  15.1 us (9%)
  between operations  13.6 us (8%)
  matrix products  11.8 us (7%)
  other arithmetic  5.74 us (3%)
    reduce_scatter x1, waiting for transfers between devices, body(): lax.psum_scatter(jnp.dot(columns, kv_weight, preferred_element_type=jnp.f...  65.1 us
    all_gather x1, waiting for transfers between devices, body(): arrived = lax.all_gather(kv_rows_local, 'blk', axis=0, tiled=True)  34.7 us
    all_to_all x1, blocking collectives, body(): lax.all_to_all(image_states, 'blk', split_axis=1, concat_axis=0, tiled=True)  27.3 us
    dot_general x2, matrix products, body(): jnp.einsum('tgrd,pgd->grtp', normed_queries, key_heads, preferred_element...  6.52 us
    slice x2, local copies, waits for them, and re-layouts, body(): key_heads = key_block[:, :kv_width].reshape(block_size, kv_heads, head_dim)  4 us
  transfers between devices with their start and end apart: 2, of which 2 were waited for; matrix products, arithmetic and copies ran while one was open for 2% of the time, Pallas kernels for 0%

commit v1 on v0

--- a/solution.py
+++ b/solution.py
@@ -5,6 +5,18 @@
 from jax.sharding import PartitionSpec as P
 
 epsilon = 1e-05
+
+
+def set_the_halves(sheet, dim_no, axis_no):
+    return jnp.concatenate(
+        lax.all_to_all(
+            jnp.stack(jnp.split(sheet, lax.axis_size("blk"), axis=dim_no), axis=0),
+            axis_name="blk",
+            split_axis=0,
+            concat_axis=0,
+        ),
+        axis=axis_no,
+    )
 
 
 def rms_norm(inputs, norm_gain):
@@ -21,7 +33,7 @@
     kv_heads = kv_width // head_dim
     query_heads = text_queries.shape[1] // head_dim
     group_size = query_heads // kv_heads
-    columns = lax.all_to_all(image_states, "blk", split_axis=1, concat_axis=0, tiled=True)
+    columns = set_the_halves(image_states, 1, 0)
     projected = lax.psum_scatter(
         jnp.dot(columns, kv_weight, preferred_element_type=jnp.float32),
         "blk",

time: 174 us -> 186 us (1.069)
  local copies, waits for them, and re-layouts: 15.1 us -> 26.7 us
    unnamed x18 -> x33, local copies, waits for them, and re-layouts: 1.5 us -> 13.6 us
where the time goes in v1:
time: 186 us; the launch traced here: 185 us
  waiting for transfers between devices  99.9 us (54%)
  blocking collectives  27.3 us (15%)
  local copies, waits for them, and re-layouts  26.7 us (14%)
  between operations  13.6 us (7%)
  matrix products  11.8 us (6%)
  other arithmetic  5.74 us (3%)
    reduce_scatter x1, waiting for transfers between devices, body(): lax.psum_scatter(jnp.dot(columns, kv_weight, preferred_element_type=jnp.f...  65.3 us
    all_gather x1, waiting for transfers between devices, body(): arrived = lax.all_gather(kv_rows_local, 'blk', axis=0, tiled=True)  34.6 us
    all_to_all x1, blocking collectives, set_the_halves(): lax.all_to_all(jnp.stack(jnp.split(sheet, lax.axis_size('blk'), axis=dim_...  27.3 us
    unnamed x33, local copies, waits for them, and re-layouts  13.6 us
    dot_general x2, matrix products, body(): jnp.einsum('tgrd,pgd->grtp', normed_queries, key_heads, preferred_element...  6.51 us
    slice x2, local copies, waits for them, and re-layouts, body(): key_heads = key_block[:, :kv_width].reshape(block_size, kv_heads, head_dim)  4 us
  transfers between devices with their start and end apart: 2, of which 2 were waited for; matrix products, arithmetic and copies ran while one was open for 2% of the time, Pallas kernels for 0%

profile of v1, /device:TPU:0, one launch (start us, length us, event | category | flops | bytes accessed | tf_op | source)
XLA Modules:
  0.0 185.0 jit_solution(4490768292273107785)
XLA Ops:
  6.5 0.9 bitcast_dynamic-update-slice_fusion.15
  7.4 0.8 bitcast_dynamic-update-slice_fusion.14
  8.2 0.8 bitcast_dynamic-update-slice_fusion.13
  9.0 0.8 bitcast_dynamic-update-slice_fusion.12
  9.8 0.8 bitcast_dynamic-update-slice_fusion.11
  11.4 0.8 bitcast_dynamic-update-slice_fusion.9
  12.2 0.8 bitcast_dynamic-update-slice_fusion.8
  13.0 0.8 bitcast_dynamic-update-slice_fusion.7
  13.8 0.8 bitcast_dynamic-update-slice_fusion.6
  14.6 0.8 bitcast_dynamic-update-slice_fusion.5
  15.5 0.8 bitcast_dynamic-update-slice_fusion.4
  16.3 0.8 bitcast_dynamic-update-slice_fusion.3
  17.1 0.8 bitcast_dynamic-update-slice_fusion.2
  17.9 0.8 bitcast_dynamic-update-slice_fusion.1
  19.5 27.3 %all_to_all.5 = bf16[16,48,512]{2,1,0:T(8,128)(2,1)S(1)} all-to-all(bf16[16,48,512]{2,1,0:T(8,128)(2,1)S(1)} %bitcast_dynamic-update-slice_fusion), channel_id=1, replica_groups=mesh['groups'=2,'blk'=16] {'blk'}, dimensions={0} | all-to-all | bytes 1572864 | tf_op jit(solution)/shard_map/all_to_all | solution.py:12
  46.8 2.6 %fusion.34 = f32[768,1024]{1,0:T(8,128)} fusion(bf16[768,512]{1,0:T(8,128)(2,1)S(1)} %bitcast.95, bf16[512,1024]{1,0:T(8,128)(2,1)S(1)} %copy-done), kind=kOutput, calls=%fused_computation.66 | convolution fusion | flops 805306368 | bytes 4980736 | tf_op jit(solution)/shard_map/dot_general | solution.py:38
  50.1 65.3 %reduce-scatter.2.cloned.1.call-done = f32[48,1024]{1,0:T(8,128)} async-done(((f32[768,1024]{1,0:T(8,128)}), f32[48,1024]{1,0:T(8,128)}) %reduce-scatter.2.cloned.1.call-update) | async-done | bytes 196624 | tf_op jit(solution)/shard_map/reduce_scatter | solution.py:37
  115.4 0.9 slice_multiply_fusion
  116.5 0.9 slice.40
  117.5 0.9 fusion.27
  120.7 1.4 convert_bitcast_fusion
  123.1 34.6 %all-gather.2.cloned.1.call-done = bf16[768,1024]{1,0:T(8,128)(2,1)} async-done(((bf16[48,1024]{1,0:T(8,128)(2,1)}), bf16[768,1024]{1,0:T(8,128)(2,1)}) %all-gather.2.cloned.1.call-update) | async-done | bytes 1572880 | tf_op jit(solution)/shard_map/all_gather | solution.py:60
  157.7 2.2 %fusion.32 = (bf16[512,512]{1,0:T(8,128)(2,1)}, bf16[512,512]{1,0:T(8,128)(2,1)}) fusion(bf16[768,1024]{1,0:T(8,128)(2,1)} %all-gather.2.cloned.1.call-done), kind=kLoop, calls=%fused_computation.64 | loop fusion | bytes 2097152 | tf_op jit(solution)/shard_map/slice | solution.py:68
  159.9 2.0 %reshape.124 = bf16[512,4,128]{2,1,0:T(4,128)(2,1)} reshape(bf16[512,512]{1,0:T(8,128)(2,1)} %get-tuple-element.5) | data formatting | bytes 1048576 | tf_op jit(solution)/shard_map/reshape | solution.py:68
  161.9 1.8 fusion.33
  164.4 1.1 copy.75
  165.5 2.0 %copy.72 = bf16[512,512]{0,1:T(8,128)(2,1)} copy(bf16[512,512]{1,0:T(8,128)(2,1)} %get-tuple-element.6) | data formatting | bytes 1048576 | tf_op jit(solution)/shard_map/reshape | solution.py:69
  167.5 3.2 %fusion.7 = (f32[4,8,128]{2,1,0:T(8,128)S(1)}, f32[4,256,128,8]{2,1,3,0:T(8,128)S(1)}) fusion(pred[128,256]{0,1:T(8,128)(4,1)S(1)} %broadcast_compare_fusion.1, f32[128,4,8,128]{3,2,1,0:T(8,128)S(1)} %bitcast.96, f32[128]{0:T(128)S(1)} %copy-done.7, f32[128,4,8]{0,2,1:T(8,128)S(1)} %rsqrt_bitcast_fusion, bf16[256,4,128,1]{2,1,0,3:T(4,128)(2,1)} %bitcast.103), kind=kOutput, calls=%fused_computation.8 | convolution fusion | flops 273149952 | bytes 6619648 | tf_op jit(solution)/shard_map/tgrd,pgd->grtp/dot_general | solution.py:76
  170.8 0.9 fusion.10
  171.8 3.3 %fusion = (f32[4,8,128]{2,1,0:T(8,128)S(1)}, f32[4,512,128,8]{2,1,3,0:T(8,128)S(1)}) fusion(pred[128,512]{0,1:T(8,128)(4,1)S(1)} %broadcast_compare_fusion, f32[128,4,8,128]{3,2,1,0:T(8,128)S(1)} %bitcast.97, f32[128]{0:T(128)S(1)} %copy-done.7, f32[128,4,8]{0,2,1:T(8,128)S(1)} %rsqrt_bitcast_fusion, bf16[512,4,128,1]{2,1,0,3:T(4,128)(2,1)S(1)} %bitcast.100), kind=kOutput, calls=%fused_computation.1 | convolution fusion | flops 544731136 | bytes 11108864 | tf_op jit(solution)/shard_map/tgrd,pgd->grtp/dot_general | solution.py:76
  175.1 1.8 fusion.12
  176.9 1.3 copy.63
  (45 shorter events, 6.6 us)
Async XLA Ops:
  6.5 40.3 %copy-start = (bf16[512,1024]{1,0:T(8,128)(2,1)S(1)}, bf16[512,1024]{1,0:T(8,128)(2,1)}, u32[]{:S(2)}) copy-start(bf16[512,1024]{1,0:T(8,128)(2,1)} %param.9) | copy-start | bytes 3145732
  6.5 108.8 %reduce-scatter.2.cloned.1.call-start = ((), (), s32[]{:S(2)}) async-start(), calls=%async_computation.2 | async-start | bytes 3342336 | tf_op jit(solution)/shard_map/reduce_scatter | solution.py:37
  49.4 0.7 copy-start.4
  49.4 69.6 %copy-start.5 = (s32[3]{0:T(128)S(1)}, s32[3]{0:T(128)}, u32[]{:S(2)}) copy-start(s32[3]{0:T(128)} %param.12) | copy-start | bytes 40
  49.4 69.8 %copy-start.6 = (s32[3]{0:T(128)S(1)}, s32[3]{0:T(128)}, u32[]{:S(2)}) copy-start(s32[3]{0:T(128)} %param.13) | copy-start | bytes 40
  49.4 70.0 %copy-start.1 = (bf16[128,4096]{1,0:T(8,128)(2,1)S(1)}, bf16[128,4096]{1,0:T(8,128)(2,1)}, u32[]{:S(2)}) copy-start(bf16[128,4096]{1,0:T(8,128)(2,1)} %param.7) | copy-start | bytes 3145732
  49.5 108.2 %all-gather.2.cloned.1.call-start = ((), (), s32[]{:S(2)}) async-start(), calls=%async_computation.3 | async-start | bytes 1671168 | tf_op jit(solution)/shard_map/all_gather | solution.py:60
  159.9 7.7 %copy-start.7 = (f32[128]{0:T(128)S(1)}, f32[128]{0:T(128)}, u32[]{:S(2)}) copy-start(f32[128]{0:T(128)} %param.10) | copy-start | bytes 1540
  170.8 1.0 copy-start.2
  171.8 3.3 %copy-start.3 = (bf16[512,512]{0,1:T(8,128)(2,1)S(1)}, bf16[512,512]{0,1:T(8,128)(2,1)}, u32[]{:S(2)}) copy-start(bf16[512,512]{0,1:T(8,128)(2,1)} %copy.72) | copy-start | bytes 1572868
Sparse Core Ops, SparseCore 0:
  49.6 65.7 reduce-scatter.1
  119.2 38.4 all-gather.1
